TPU v7x, 512 devices: a whole 4x8x8 slice. The times are simulated.
512 devices in a mesh: grp: 8 (over y), dev: 64 (over z, x, core).
Axes of the slice: x: 4, y: 8, z: 8, core: 2. Of those that a mesh axis runs over, the one named last changes fastest.
Arguments:
- leaf_right: float32 [32, 131072], P(None, ('grp', 'dev')), may hold values from -6 to 6
- leaf_inverse: float32 [1024, 128, 128], P(('grp', 'dev')), may hold values from -1 to 2, as said below
- leaf_link: float32 [1024, 128, 128], P(('grp', 'dev')), may hold values from -0.25 to 0.25
- leaf_front: float32 [1024, 128, 128], P(('grp', 'dev')), may hold values from -0.1875 to 0.1875
- parents: int32 [1024], P(('grp', 'dev')), may hold values from 1 to 2, as said below
- front_rows: int32 [1024], P(('grp', 'dev')), may hold values from 0 to 15
- live_blocks: int32 [512], P(('grp', 'dev')), may hold values from 1 to 2, 896 in all
- front_right: float32 [32, 16384], P(None, ('grp', 'dev')), may hold values from -6 to 6
- front_inverse: float32 [16384, 2048], P(('grp', 'dev')), may hold values from -1 to 2, as said below
- front_couple: float32 [16384, 4096], P(('grp', 'dev')), may hold values from -0.046875 to 0.046875
- root_right: float32 [32, 2, 2048], P(None, None, 'dev'), may hold values from -6 to 6
- root_inverse: float32 [2, 2048, 2048], P(None, 'dev', 'grp'), may hold values from -1 to 2, as said below
- root_couple: float32 [1, 2048, 2048], P(None, 'dev', 'grp'), may hold values from -0.09375 to 0.09375
Outputs:
- leaf_solution: float32 [32, 131072], P(None, ('grp', 'dev'))
- front_solution: float32 [32, 16384], P(None, 'grp')
- root_solution: float32 [32, 2, 2048], P(None, None, 'dev')
Inputs may be any that keep to these rules, and one draw needn't show every extreme that they name: For local block k = b mod 2, parents[b] lies in k + 1 .. 2; the value 2 means no parent among the piece's blocks. A piece's live blocks are its first live_blocks[p]; some piece has all 2. `leaf_inverse`: each block is lower triangular with a positive diagonal. `front_inverse`: each front's block is lower triangular with a positive diagonal. `root_inverse`: each level's block is lower triangular with a positive diagonal.
All inputs are finite; a program needn't handle non-finite values.
Results may differ from a plain program's by a relative error of at most 0.0003.
Values sent between devices are 32-bit elements; how exact they have to be, the bound alone decides.
No kernel may reach another device: no remote copies, remote signals or barrier semaphores. Data moves between devices by JAX's collectives and lax.ppermute only.
A program may use at most 64 MiB of HBM per device.

v0:
```python
import jax
import jax.numpy as jnp
from jax import lax
from jax.sharding import Mesh
from jax.sharding import PartitionSpec as P

EXACT = lax.Precision.HIGH
NEAR = ("x", "core")
DEV = ("z", "x", "core")


def mm(left, right):
    return jnp.dot(left, right, precision=EXACT)


def mmt(left, right):
    return jnp.einsum("rn,mn->rm", left, right, precision=EXACT)


def swap(chunks, axes):
    return lax.all_to_all(chunks, axes, 0, 0, tiled=True)


def spread(values, axes, count):
    return swap(jnp.broadcast_to(values[None], (count,) + values.shape), axes)


def reduce_over(values, axes, count):
    return jnp.sum(spread(values, axes, count), 0)


def make_body(sizes):
    n_grp, n_z = (sizes["grp"], sizes["z"])
    n_near = sizes["x"] * sizes["core"]
    n_dev = n_z * n_near

    def body(
        leaf_right,
        leaf_inverse,
        leaf_link,
        leaf_front,
        parents,
        front_rows,
        live_blocks,
        front_right,
        front_inverse,
        front_couple,
        root_right,
        root_inverse,
        root_couple,
    ):
        rows = leaf_right.shape[0]
        width = leaf_inverse.shape[1]
        front_order = front_inverse.shape[1]
        n_front = front_order // width
        share = front_inverse.shape[0]
        slab = share * n_z
        part = root_inverse.shape[2]
        live = live_blocks[0]
        my_z = lax.axis_index("z")

        def near_sum(natural):
            chunks = natural.reshape(rows, n_z, n_near, share).transpose(2, 0, 1, 3)
            return jnp.sum(swap(chunks.reshape(n_near, rows, slab), NEAR), 0)

        def own(values):
            return lax.dynamic_slice_in_dim(values, my_z * share, share, 1)

        blocks = front_inverse.reshape(share, n_z, part).transpose(1, 0, 2)
        wide = jnp.concatenate([blocks, root_inverse, root_couple], 0)
        wide = lax.all_gather(wide, "z", axis=1, tiled=True)
        front_slab, w_low, w_high, link = (wide[:n_z], wide[n_z], wide[n_z + 1], wide[n_z + 2])
        has_parent = parents[0] < live
        right0, right1 = (leaf_right[:, :width], leaf_right[:, width:])
        solved0 = jnp.where(live > 0, mm(right0, leaf_inverse[0]), 0.0)
        lifted = jnp.where(has_parent, mm(solved0, leaf_link[0]), 0.0)
        solved1 = jnp.where(live > 1, mm(right1 - lifted, leaf_inverse[1]), 0.0)
        given0, given1 = (mm(solved0, leaf_front[0]), mm(solved1, leaf_front[1]))
        slots = jnp.arange(n_front, dtype=jnp.int32)[None, :, None]
        placed = jnp.where(slots == front_rows[0], given0[:, None, :], 0.0) + jnp.where(
            slots == front_rows[1], given1[:, None, :], 0.0
        )
        update = near_sum(placed.reshape(rows, front_order))
        here = (jnp.arange(slab, dtype=jnp.int32) // share == my_z)[None, :]
        start = jnp.where(here, jnp.tile(front_right, (1, n_z)), 0.0) - update
        start = jnp.broadcast_to(reduce_over(start, "z", n_z)[None], (n_z, rows, slab))
        terms = jnp.einsum("zrk,zkn->zrn", start, front_slab, precision=EXACT)
        terms = lax.optimization_barrier(terms).reshape(n_z, rows, n_near, share)
        terms = terms.transpose(2, 1, 0, 3).reshape(n_near, rows, slab)
        y_slab = jnp.sum(swap(terms, NEAR), 0)
        y_own = own(y_slab)
        raised = mm(y_own, front_couple)
        half = rows // 2
        chunks = raised.reshape(2, half, 2, n_dev, share).transpose(3, 1, 0, 2, 4)
        raised = jnp.sum(swap(chunks.reshape(n_dev, half, 4 * share), DEV), 0)
        given = root_right.reshape(2, half, 2, share).transpose(1, 0, 2, 3).reshape(half, 4 * share)
        given = jnp.where(lax.axis_index("grp") == 0, given, 0.0) - raised
        given = jnp.sum(
            spread(given, ("grp", "z"), n_grp * n_z).reshape(n_grp, n_z, half, 4 * share), 0
        )
        given = (
            given.reshape(n_z, half, 2, 2, share).transpose(3, 2, 1, 0, 4).reshape(2, rows, slab)
        )
        low, high = (given[0], given[1])
        y_high = reduce_over(mm(high, w_high), NEAR, n_near)
        low = low - reduce_over(mmt(y_high, link), "grp", n_grp)
        y_low = reduce_over(mm(low, w_low), NEAR, n_near)
        x_low = reduce_over(mmt(y_low, w_low), "grp", n_grp)
        y_high = y_high - reduce_over(mm(x_low, link), NEAR, n_near)
        x_high = reduce_over(mmt(y_high, w_high), "grp", n_grp)
        both = jnp.concatenate([x_low, x_high], 1)
        whole = spread(both, NEAR, n_near).reshape(n_near, rows, 2, n_z, share)
        whole = whole.transpose(1, 2, 3, 0, 4).reshape(rows, 2 * front_order)
        rest = y_own - mmt(whole, front_couple)
        rest = rest.reshape(4, rows // 4, share).transpose(1, 0, 2).reshape(rows // 4, 4 * share)
        rest = spread(rest, DEV, n_dev).reshape(n_dev, rows // 4, 4, share)
        rest = rest.reshape(n_z, n_near, rows // 4, 4, share)
        rest = rest.transpose(0, 3, 2, 1, 4).reshape(n_z, rows, part)
        solved = jnp.einsum("zrn,zkn->zrk", rest, front_slab, precision=EXACT)
        front_solution = spread(jnp.sum(solved, 0), NEAR, n_near)
        front_solution = front_solution.reshape(n_near, rows, n_z, share)
        front_solution = front_solution.transpose(1, 2, 0, 3).reshape(rows, front_order)

        def back(solved, block):
            picked = lax.dynamic_slice(
                front_solution, (0, front_rows[block] * width), (rows, width)
            )
            return solved - mmt(picked, leaf_front[block])

        base0, base1 = (back(solved0, 0), back(solved1, 1))
        leaf1 = jnp.where(live > 1, mmt(base1, leaf_inverse[1]), 0.0)
        carried = jnp.where(has_parent, mmt(leaf1, leaf_link[0]), 0.0)
        leaf0 = jnp.where(live > 0, mmt(base0 - carried, leaf_inverse[0]), 0.0)
        leaf_solution = jnp.concatenate([leaf0, leaf1], 1)
        return (leaf_solution, front_solution, jnp.stack([own(x_low), own(x_high)], 1))

    return body


def solution(mesh):
    n_grp, n_dev = (mesh.shape["grp"], mesh.shape["dev"])
    fine = Mesh(mesh.devices.reshape(n_grp, n_dev // 8, 4, 2), ("grp", "z", "x", "core"))
    every = ("grp",) + DEV
    in_specs = (
        P(None, every),
        P(every, None, None),
        P(every, None, None),
        P(every, None, None),
        P(every),
        P(every),
        P(every),
        P(None, every),
        P(every, None),
        P(every, None),
        P(None, None, DEV),
        P(None, DEV, "grp"),
        P(None, DEV, "grp"),
    )
    out_specs = (P(None, every), P(None, "grp"), P(None, None, DEV))
    body = make_body(dict(fine.shape))
    return jax.shard_map(body, mesh=fine, in_specs=in_specs, out_specs=out_specs, check_vma=False)
```

profile of v0, /device:TPU:1, one launch (start us, length us, event | category | flops | bytes accessed | tf_op | source)
XLA Modules:
  0.0 311.3 jit_solution(14920914953933961020)
XLA Ops:
  20.5 10.2 %all-to-all-start = ((f32[8,32,256]{2,1,0:T(8,128)}), f32[8,32,256]{2,1,0:T(8,128)S(1)}, u32[]{:S(2)}, u32[]{:S(2)}) async-start(f32[8,32,256]{2,1,0:T(8,128)} %reshape.150), calls=%async_computation | async-start | bytes 524288 | tf_op jit(solution)/shard_map/all_to_all | solution.py:21
  30.7 6.4 %all-to-all-done = f32[8,32,256]{2,1,0:T(8,128)S(1)} async-done(((f32[8,32,256]{2,1,0:T(8,128)}), f32[8,32,256]{2,1,0:T(8,128)S(1)}, u32[]{:S(2)}, u32[]{:S(2)}) %all-to-all-start) | async-done | bytes 262176 | tf_op jit(solution)/shard_map/all_to_all | solution.py:21
  37.2 20.2 %all_to_all.70 = f32[8,32,256]{2,1,0:T(8,128)S(1)} all-to-all(f32[8,32,256]{2,1,0:T(8,128)S(1)} %broadcast_in_dim.159), channel_id=1, replica_groups=mesh['grp'=8,'z'=8,'x'=4,'core'=2] {'z'}, dimensions={0} | all-to-all | bytes 524288 | tf_op jit(solution)/shard_map/all_to_all | solution.py:21
  57.5 8.6 %all-gather.2.cloned.1.call-done = f32[11,256,256]{2,1,0:T(8,128)} async-done(((f32[11,32,256]{2,1,0:T(8,128)}), f32[11,256,256]{2,1,0:T(8,128)}) %all-gather.2.cloned.1.call-update) | async-done | bytes 2883600 | tf_op jit(solution)/shard_map/all_gather | solution.py:71
  70.3 6.6 %all-to-all-start.2 = ((f32[8,32,256]{2,1,0:T(8,128)}), f32[8,32,256]{2,1,0:T(8,128)S(1)}, u32[]{:S(2)}, u32[]{:S(2)}) async-start(f32[8,32,256]{2,1,0:T(8,128)} %reshape.153), calls=%async_computation.2 | async-start | bytes 524288 | tf_op jit(solution)/shard_map/all_to_all | solution.py:21
  76.9 6.5 %all-to-all-done.2 = f32[8,32,256]{2,1,0:T(8,128)S(1)} async-done(((f32[8,32,256]{2,1,0:T(8,128)}), f32[8,32,256]{2,1,0:T(8,128)S(1)}, u32[]{:S(2)}, u32[]{:S(2)}) %all-to-all-start.2) | async-done | bytes 262176 | tf_op jit(solution)/shard_map/all_to_all | solution.py:21
  88.5 6.7 %all-to-all-start.3 = ((f32[64,16,128]{2,1,0:T(8,128)}), f32[64,16,128]{2,1,0:T(8,128)}, u32[]{:S(2)}, u32[]{:S(2)}) async-start(f32[64,16,128]{2,1,0:T(8,128)} %copy.75), calls=%async_computation.3 | async-start | bytes 1048576 | tf_op jit(solution)/shard_map/all_to_all | solution.py:21
  95.3 17.5 %all-to-all-done.3 = f32[64,16,128]{2,1,0:T(8,128)} async-done(((f32[64,16,128]{2,1,0:T(8,128)}), f32[64,16,128]{2,1,0:T(8,128)}, u32[]{:S(2)}, u32[]{:S(2)}) %all-to-all-start.3) | async-done | bytes 524320 | tf_op jit(solution)/shard_map/all_to_all | solution.py:21
  114.0 25.6 %all_to_all.71 = f32[64,16,128]{2,1,0:T(8,128)} all-to-all(f32[64,16,128]{2,1,0:T(8,128)S(1)} %broadcast_in_dim.162), channel_id=1, replica_groups=mesh['grp'=8,'z'=8,'x'=4,'core'=2] {'grp','z'}, dimensions={0} | all-to-all | bytes 1048576 | tf_op jit(solution)/shard_map/all_to_all | solution.py:21
  145.1 13.3 %all_to_all.72 = f32[8,32,256]{2,1,0:T(8,128)} all-to-all(f32[8,32,256]{2,1,0:T(8,128)S(1)} %broadcast_in_dim.163), channel_id=1, replica_groups=mesh['grp'=8,'z'=8,'x'=4,'core'=2] {'x','core'}, dimensions={0} | all-to-all | bytes 524288 | tf_op jit(solution)/shard_map/all_to_all | solution.py:21
  159.7 13.9 %all_to_all.73 = f32[8,32,256]{2,1,0:T(8,128)} all-to-all(f32[8,32,256]{2,1,0:T(8,128)S(1)} %broadcast_in_dim.164), channel_id=1, replica_groups=mesh['grp'=8,'z'=8,'x'=4,'core'=2] {'grp'}, dimensions={0} | all-to-all | bytes 524288 | tf_op jit(solution)/shard_map/all_to_all | solution.py:21
  178.8 12.2 %all_to_all.74 = f32[8,32,256]{2,1,0:T(8,128)} all-to-all(f32[8,32,256]{2,1,0:T(8,128)S(1)} %broadcast_in_dim.165), channel_id=1, replica_groups=mesh['grp'=8,'z'=8,'x'=4,'core'=2] {'x','core'}, dimensions={0} | all-to-all | bytes 524288 | tf_op jit(solution)/shard_map/all_to_all | solution.py:21
  192.3 13.4 %all_to_all.75 = f32[8,32,256]{2,1,0:T(8,128)} all-to-all(f32[8,32,256]{2,1,0:T(8,128)S(1)} %broadcast_in_dim.166), channel_id=1, replica_groups=mesh['grp'=8,'z'=8,'x'=4,'core'=2] {'grp'}, dimensions={0} | all-to-all | bytes 524288 | tf_op jit(solution)/shard_map/all_to_all | solution.py:21
  206.8 12.0 %all_to_all.76 = f32[8,32,256]{2,1,0:T(8,128)} all-to-all(f32[8,32,256]{2,1,0:T(8,128)S(1)} %broadcast_in_dim.167), channel_id=1, replica_groups=mesh['grp'=8,'z'=8,'x'=4,'core'=2] {'x','core'}, dimensions={0} | all-to-all | bytes 524288 | tf_op jit(solution)/shard_map/all_to_all | solution.py:21
  220.2 13.4 %all_to_all.77 = f32[8,32,256]{2,1,0:T(8,128)} all-to-all(f32[8,32,256]{2,1,0:T(8,128)S(1)} %broadcast_in_dim.168), channel_id=1, replica_groups=mesh['grp'=8,'z'=8,'x'=4,'core'=2] {'grp'}, dimensions={0} | all-to-all | bytes 524288 | tf_op jit(solution)/shard_map/all_to_all | solution.py:21
  234.6 14.9 %all_to_all.78 = f32[8,32,512]{2,1,0:T(8,128)} all-to-all(f32[8,32,512]{2,1,0:T(8,128)S(1)} %broadcast_in_dim.169), channel_id=1, replica_groups=mesh['grp'=8,'z'=8,'x'=4,'core'=2] {'x','core'}, dimensions={0} | all-to-all | bytes 1048576 | tf_op jit(solution)/shard_map/all_to_all | solution.py:21
  249.5 2.8 reshape.158
  252.3 4.1 %copy.77 = f32[32,2,8,8,32]{4,3,2,1,0:T(8,128)} copy(f32[32,2,8,8,32]{4,2,1,0,3:T(8,128)} %bitcast.110) | data formatting | bytes 1048576 | tf_op jit(solution)/shard_map/transpose | solution.py:113
  256.4 3.3 %reshape.159 = f32[32,4096]{1,0:T(8,128)} reshape(f32[32,2,8,8,32]{4,3,2,1,0:T(8,128)} %copy.77) | data formatting | bytes 1048576 | tf_op jit(solution)/shard_map/reshape | solution.py:113
  262.0 5.9 %all-to-all-start.12 = ((f32[64,8,128]{2,1,0:T(8,128)}), f32[64,8,128]{2,1,0:T(8,128)}, u32[]{:S(2)}, u32[]{:S(2)}) async-start(f32[64,8,128]{2,1,0:T(8,128)} %broadcast_in_dim.171), calls=%async_computation.12 | async-start | bytes 524288 | tf_op jit(solution)/shard_map/all_to_all | solution.py:21
  269.3 11.7 %all-to-all-done.12 = f32[64,8,128]{2,1,0:T(8,128)} async-done(((f32[64,8,128]{2,1,0:T(8,128)}), f32[64,8,128]{2,1,0:T(8,128)}, u32[]{:S(2)}, u32[]{:S(2)}) %all-to-all-start.12) | async-done | bytes 262176 | tf_op jit(solution)/shard_map/all_to_all | solution.py:21
  283.3 2.9 copy.79
  291.2 3.8 %all-to-all-start.13 = ((f32[8,32,256]{2,1,0:T(8,128)}), f32[8,32,256]{2,1,0:T(8,128)S(1)}, u32[]{:S(2)}, u32[]{:S(2)}) async-start(f32[8,32,256]{2,1,0:T(8,128)} %broadcast_in_dim.172), calls=%async_computation.13 | async-start | bytes 524288 | tf_op jit(solution)/shard_map/all_to_all | solution.py:21
  295.8 5.7 %all-to-all-done.13 = f32[8,32,256]{2,1,0:T(8,128)S(1)} async-done(((f32[8,32,256]{2,1,0:T(8,128)}), f32[8,32,256]{2,1,0:T(8,128)S(1)}, u32[]{:S(2)}, u32[]{:S(2)}) %all-to-all-start.13) | async-done | bytes 262176 | tf_op jit(solution)/shard_map/all_to_all | solution.py:21
  (125 shorter events, 52.5 us)
Async XLA Ops:
  7.2 76.2 %copy-start = (f32[32,4096]{1,0:T(8,128)S(1)}, f32[32,4096]{1,0:T(8,128)}, u32[]{:S(2)}) copy-start(f32[32,4096]{1,0:T(8,128)} %param.22) | copy-start | bytes 1572868
  7.2 11.3 %copy-start.3 = (f32[2,128,128]{2,1,0:T(8,128)S(1)}, f32[2,128,128]{2,1,0:T(8,128)}, u32[]{:S(2)}) copy-start(f32[2,128,128]{2,1,0:T(8,128)} %param.16) | copy-start | bytes 393220
  7.2 59.0 %all-gather.2.cloned.1.call-start = ((), (), s32[]{:S(2)}) async-start(), calls=%async_computation.14 | async-start | bytes 3244032 | tf_op jit(solution)/shard_map/all_gather | solution.py:71
  17.2 1.0 copy-start.9
  19.0 11.6 %copy-start.15 = (f32[32,32]{1,0:T(8,128)S(1)}, f32[32,32]{1,0:T(8,128)}, u32[]{:S(2)}) copy-start(f32[32,32]{1,0:T(8,128)} %param.20) | copy-start | bytes 12292
  20.5 16.7 %all-to-all-start = ((f32[8,32,256]{2,1,0:T(8,128)}), f32[8,32,256]{2,1,0:T(8,128)S(1)}, u32[]{:S(2)}, u32[]{:S(2)}) async-start(f32[8,32,256]{2,1,0:T(8,128)} %reshape.150), calls=%async_computation | async-start | bytes 524288 | tf_op jit(solution)/shard_map/all_to_all | solution.py:21
  70.3 13.1 %all-to-all-start.2 = ((f32[8,32,256]{2,1,0:T(8,128)}), f32[8,32,256]{2,1,0:T(8,128)S(1)}, u32[]{:S(2)}, u32[]{:S(2)}) async-start(f32[8,32,256]{2,1,0:T(8,128)} %reshape.153), calls=%async_computation.2 | async-start | bytes 524288 | tf_op jit(solution)/shard_map/all_to_all | solution.py:21
  83.4 2.7 copy-start.11
  84.5 10.7 %copy-start.14 = (f32[32,2,32]{2,1,0:T(2,128)S(1)}, f32[32,2,32]{2,1,0:T(2,128)}, u32[]{:S(2)}) copy-start(f32[32,2,32]{2,1,0:T(2,128)} %param.23) | copy-start | bytes 24580
  88.5 55.6 %copy-start.1 = (f32[11,256,256]{2,1,0:T(8,128)S(1)}, f32[11,256,256]{2,1,0:T(8,128)}, u32[]{:S(2)}) copy-start(f32[11,256,256]{2,1,0:T(8,128)} %all-gather.2.cloned.1.call-done) | copy-start | bytes 8650756
  88.5 24.3 %all-to-all-start.3 = ((f32[64,16,128]{2,1,0:T(8,128)}), f32[64,16,128]{2,1,0:T(8,128)}, u32[]{:S(2)}, u32[]{:S(2)}) async-start(f32[64,16,128]{2,1,0:T(8,128)} %copy.75), calls=%async_computation.3 | async-start | bytes 1048576 | tf_op jit(solution)/shard_map/all_to_all | solution.py:21
  142.7 0.7 copy-start.2
  159.4 14.2 %copy-start.7 = (f32[32,256]{1,0:T(8,128)}, f32[32,256]{1,0:T(8,128)S(1)}, u32[]{:S(2)}) copy-start(f32[32,256]{1,0:T(8,128)S(1)} %reduce_sum.110) | copy-start | bytes 98308
  177.6 42.3 %copy-start.8 = (f32[32,256]{1,0:T(8,128)S(1)}, f32[32,256]{1,0:T(8,128)}, u32[]{:S(2)}) copy-start(f32[32,256]{1,0:T(8,128)} %copy-done.7) | copy-start | bytes 98308
  252.3 7.4 %copy-start.12 = (f32[32,256]{1,0:T(8,128)S(1)}, f32[32,256]{1,0:T(8,128)}, u32[]{:S(2)}) copy-start(f32[32,256]{1,0:T(8,128)} %copy-done.11) | copy-start | bytes 98308
  262.0 19.0 %all-to-all-start.12 = ((f32[64,8,128]{2,1,0:T(8,128)}), f32[64,8,128]{2,1,0:T(8,128)}, u32[]{:S(2)}, u32[]{:S(2)}) async-start(f32[64,8,128]{2,1,0:T(8,128)} %broadcast_in_dim.171), calls=%async_computation.12 | async-start | bytes 524288 | tf_op jit(solution)/shard_map/all_to_all | solution.py:21
  290.4 12.4 %copy-start.4 = (f32[2,128,128]{2,1,0:T(8,128)S(1)}, f32[2,128,128]{2,1,0:T(8,128)}, u32[]{:S(2)}) copy-start(f32[2,128,128]{2,1,0:T(8,128)} %param.16) | copy-start | bytes 393220
  290.4 12.4 %copy-start.10 = (f32[32,128]{1,0:T(8,128)S(1)}, f32[32,128]{1,0:T(8,128)}, u32[]{:S(2)}) copy-start(f32[32,128]{1,0:T(8,128)} %copy-done.9) | copy-start | bytes 49156
  290.5 12.6 %copy-start.5 = (f32[2,128,128]{2,1,0:T(8,128)S(1)}, f32[2,128,128]{2,1,0:T(8,128)}, u32[]{:S(2)}) copy-start(f32[2,128,128]{2,1,0:T(8,128)} %param.14) | copy-start | bytes 393220
  291.2 12.2 %copy-start.13 = (f32[2,128,128]{2,1,0:T(8,128)S(1)}, f32[2,128,128]{2,1,0:T(8,128)}, u32[]{:S(2)}) copy-start(f32[2,128,128]{2,1,0:T(8,128)} %param.15) | copy-start | bytes 393220
  291.2 10.2 %all-to-all-start.13 = ((f32[8,32,256]{2,1,0:T(8,128)}), f32[8,32,256]{2,1,0:T(8,128)S(1)}, u32[]{:S(2)}, u32[]{:S(2)}) async-start(f32[8,32,256]{2,1,0:T(8,128)} %broadcast_in_dim.172), calls=%async_computation.13 | async-start | bytes 524288 | tf_op jit(solution)/shard_map/all_to_all | solution.py:21
  302.8 1.6 copy-start.6
Sparse Core Ops, SparseCore 0:
  10.1 56.0 all-gather.1
where the time goes:
time: 313 us; the launch traced here: 311 us
  blocking collectives  139 us (44%)
  waiting for transfers between devices  56.3 us (18%)
  local copies, waits for them, and re-layouts  37.6 us (12%)
  starting transfers between devices  33.2 us (11%)
  between operations  17.3 us (6%)
  other arithmetic  14.9 us (5%)
  matrix products  13 us (4%)
    all_to_all x9, blocking collectives, swap(): return lax.all_to_all(chunks, axes, 0, 0, tiled=True)  139 us
    all_to_all x5, waiting for transfers between devices, swap(): return lax.all_to_all(chunks, axes, 0, 0, tiled=True)  47.7 us
    all_to_all x5, starting transfers between devices, swap(): return lax.all_to_all(chunks, axes, 0, 0, tiled=True)  33.1 us
    all_gather x1, waiting for transfers between devices, body(): wide = lax.all_gather(wide, 'z', axis=1, tiled=True)  8.64 us
    reduce_sum x7, other arithmetic, reduce_over(): return jnp.sum(spread(values, axes, count), 0)  6.46 us
  transfers between devices with their start and end apart: 6, of which 6 were waited for; matrix products, arithmetic and copies ran while one was open for 3% of the time, Pallas kernels for 0%

commit v1 on v0

--- a/solution.py
+++ b/solution.py
@@ -3,6 +3,7 @@
 from jax import lax
 from jax.sharding import Mesh
 from jax.sharding import PartitionSpec as P
+from jax.lax import all_to_all, axis_size
 
 EXACT = lax.Precision.HIGH
 NEAR = ("x", "core")
@@ -68,7 +69,10 @@
 
         blocks = front_inverse.reshape(share, n_z, part).transpose(1, 0, 2)
         wide = jnp.concatenate([blocks, root_inverse, root_couple], 0)
-        wide = lax.all_gather(wide, "z", axis=1, tiled=True)
+        w1 = axis_size("z")
+        taken_in = jnp.stack([wide] * w1)
+        e_next = all_to_all(taken_in, "z", split_axis=0, concat_axis=0)
+        wide = jnp.concatenate(e_next, axis=1)
         front_slab, w_low, w_high, link = (wide[:n_z], wide[n_z], wide[n_z + 1], wide[n_z + 2])
         has_parent = parents[0] < live
         right0, right1 = (leaf_right[:, :width], leaf_right[:, width:])

time: 313 us -> 355 us (1.13)
  waiting for transfers between devices: 56.3 us -> 138 us
  blocking collectives: 139 us -> 91.2 us
  starting transfers between devices: 33.2 us -> 52.3 us
  between operations: 17.3 us -> 3.84 us
  local copies, waits for them, and re-layouts: 37.6 us -> 47 us
  other arithmetic: 14.9 us -> 10.2 us
    all_to_all x0 -> x1, waiting for transfers between devices: none -> 64.8 us  [body(): e_next = all_to_all(taken_in, 'z', split_axis=0, concat_axis=0)]
    all_to_all x9 -> x7, blocking collectives: 139 us -> 91.2 us  [swap(): return lax.all_to_all(chunks, axes, 0, 0, tiled=True)]
    all_to_all x5 -> x7, waiting for transfers between devices: 47.7 us -> 73.2 us  [swap(): return lax.all_to_all(chunks, axes, 0, 0, tiled=True)]
    all_to_all x5 -> x7, starting transfers between devices: 33.1 us -> 47.9 us  [swap(): return lax.all_to_all(chunks, axes, 0, 0, tiled=True)]
    all_gather x1 -> x0, waiting for transfers between devices: 8.64 us -> none  [body(): wide = lax.all_gather(wide, 'z', axis=1, tiled=True)]
    all_to_all x0 -> x1, starting transfers between devices: none -> 4.41 us  [body(): e_next = all_to_all(taken_in, 'z', split_axis=0, concat_axis=0)]
  transfers between devices with their start and end apart: 6 -> 8, of which waited for: 6 -> 8; matrix products, arithmetic and copies ran while one was open for 3% -> 1% of each run, Pallas kernels for 0% -> 0%
where the time goes in v1:
time: 355 us; the launch traced here: 353 us
  waiting for transfers between devices  138 us (39%)
  blocking collectives  91.2 us (26%)
  starting transfers between devices  52.3 us (15%)
  local copies, waits for them, and re-layouts  47 us (13%)
  matrix products  10.3 us (3%)
  other arithmetic  10.2 us (3%)
  between operations  3.84 us (1%)
    all_to_all x7, blocking collectives, swap(): return lax.all_to_all(chunks, axes, 0, 0, tiled=True)  91.2 us
    all_to_all x7, waiting for transfers between devices, swap(): return lax.all_to_all(chunks, axes, 0, 0, tiled=True)  73.2 us
    all_to_all x1, waiting for transfers between devices, body(): e_next = all_to_all(taken_in, 'z', split_axis=0, concat_axis=0)  64.8 us
    all_to_all x7, starting transfers between devices, swap(): return lax.all_to_all(chunks, axes, 0, 0, tiled=True)  47.9 us
  transfers between devices with their start and end apart: 8, of which 8 were waited for; matrix products, arithmetic and copies ran while one was open for 1% of the time, Pallas kernels for 0%

profile of v1, /device:TPU:1, one launch (start us, length us, event | category | flops | bytes accessed | tf_op | source)
XLA Modules:
  0.0 352.8 jit_solution(8247963099260739278)
XLA Ops:
  11.8 10.2 %all-to-all-start = ((f32[8,32,256]{2,1,0:T(8,128)}), f32[8,32,256]{2,1,0:T(8,128)S(1)}, u32[]{:S(2)}, u32[]{:S(2)}) async-start(f32[8,32,256]{2,1,0:T(8,128)} %reshape.163), calls=%async_computation | async-start | bytes 524288 | tf_op jit(solution)/shard_map/all_to_all | solution.py:22
  22.1 6.4 %all-to-all-done = f32[8,32,256]{2,1,0:T(8,128)S(1)} async-done(((f32[8,32,256]{2,1,0:T(8,128)}), f32[8,32,256]{2,1,0:T(8,128)S(1)}, u32[]{:S(2)}, u32[]{:S(2)}) %all-to-all-start) | async-done | bytes 262176 | tf_op jit(solution)/shard_map/all_to_all | solution.py:22
  29.2 5.6 %all-to-all-start.1 = ((f32[8,32,256]{2,1,0:T(8,128)}), f32[8,32,256]{2,1,0:T(8,128)S(1)}, u32[]{:S(2)}, u32[]{:S(2)}) async-start(f32[8,32,256]{2,1,0:T(8,128)} %broadcast_in_dim.159), calls=%async_computation.1 | async-start | bytes 524288 | tf_op jit(solution)/shard_map/all_to_all | solution.py:22
  34.9 10.1 %all-to-all-done.1 = f32[8,32,256]{2,1,0:T(8,128)S(1)} async-done(((f32[8,32,256]{2,1,0:T(8,128)}), f32[8,32,256]{2,1,0:T(8,128)S(1)}, u32[]{:S(2)}, u32[]{:S(2)}) %all-to-all-start.1) | async-done | bytes 262176 | tf_op jit(solution)/shard_map/all_to_all | solution.py:22
  47.0 4.4 %all-to-all-start.2 = ((f32[8,11,32,256]{3,2,1,0:T(8,128)}), f32[8,11,32,256]{3,2,1,0:T(8,128)}, u32[]{:S(2)}, u32[]{:S(2)}) async-start(f32[8,11,32,256]{3,2,1,0:T(8,128)} %stack.8), calls=%async_computation.2 | async-start | bytes 5767168 | tf_op jit(solution)/shard_map/all_to_all | solution.py:74
  51.5 64.8 %all-to-all-done.2 = f32[8,11,32,256]{3,2,1,0:T(8,128)} async-done(((f32[8,11,32,256]{3,2,1,0:T(8,128)}), f32[8,11,32,256]{3,2,1,0:T(8,128)}, u32[]{:S(2)}, u32[]{:S(2)}) %all-to-all-start.2) | async-done | bytes 2883616 | tf_op jit(solution)/shard_map/all_to_all | solution.py:74
  125.1 7.5 %all-to-all-start.3 = ((f32[8,32,256]{2,1,0:T(8,128)}), f32[8,32,256]{2,1,0:T(8,128)S(1)}, u32[]{:S(2)}, u32[]{:S(2)}) async-start(f32[8,32,256]{2,1,0:T(8,128)} %reshape.167), calls=%async_computation.3 | async-start | bytes 524288 | tf_op jit(solution)/shard_map/all_to_all | solution.py:22
  132.7 6.5 %all-to-all-done.3 = f32[8,32,256]{2,1,0:T(8,128)S(1)} async-done(((f32[8,32,256]{2,1,0:T(8,128)}), f32[8,32,256]{2,1,0:T(8,128)S(1)}, u32[]{:S(2)}, u32[]{:S(2)}) %all-to-all-start.3) | async-done | bytes 262176 | tf_op jit(solution)/shard_map/all_to_all | solution.py:22
  147.2 5.1 %all-to-all-start.4 = ((f32[64,16,128]{2,1,0:T(8,128)}), f32[64,16,128]{2,1,0:T(8,128)S(1)}, u32[]{:S(2)}, u32[]{:S(2)}) async-start(f32[64,16,128]{2,1,0:T(8,128)} %copy.85), calls=%async_computation.4 | async-start | bytes 1048576 | tf_op jit(solution)/shard_map/all_to_all | solution.py:22
  152.5 17.6 %all-to-all-done.4 = f32[64,16,128]{2,1,0:T(8,128)S(1)} async-done(((f32[64,16,128]{2,1,0:T(8,128)}), f32[64,16,128]{2,1,0:T(8,128)S(1)}, u32[]{:S(2)}, u32[]{:S(2)}) %all-to-all-start.4) | async-done | bytes 524320 | tf_op jit(solution)/shard_map/all_to_all | solution.py:22
  171.1 10.0 %all-to-all-start.5 = ((f32[64,16,128]{2,1,0:T(8,128)}), f32[64,16,128]{2,1,0:T(8,128)}, u32[]{:S(2)}, u32[]{:S(2)}) async-start(f32[64,16,128]{2,1,0:T(8,128)} %broadcast_in_dim.162), calls=%async_computation.5 | async-start | bytes 1048576 | tf_op jit(solution)/shard_map/all_to_all | solution.py:22
  182.3 15.1 %all-to-all-done.5 = f32[64,16,128]{2,1,0:T(8,128)} async-done(((f32[64,16,128]{2,1,0:T(8,128)}), f32[64,16,128]{2,1,0:T(8,128)}, u32[]{:S(2)}, u32[]{:S(2)}) %all-to-all-start.5) | async-done | bytes 524320 | tf_op jit(solution)/shard_map/all_to_all | solution.py:22
  202.9 13.3 %all_to_all.75 = f32[8,32,256]{2,1,0:T(8,128)} all-to-all(f32[8,32,256]{2,1,0:T(8,128)S(1)} %broadcast_in_dim.163), channel_id=1, replica_groups=mesh['grp'=8,'z'=8,'x'=4,'core'=2] {'x','core'}, dimensions={0} | all-to-all | bytes 524288 | tf_op jit(solution)/shard_map/all_to_all | solution.py:22
  217.5 13.9 %all_to_all.76 = f32[8,32,256]{2,1,0:T(8,128)} all-to-all(f32[8,32,256]{2,1,0:T(8,128)S(1)} %broadcast_in_dim.164), channel_id=1, replica_groups=mesh['grp'=8,'z'=8,'x'=4,'core'=2] {'grp'}, dimensions={0} | all-to-all | bytes 524288 | tf_op jit(solution)/shard_map/all_to_all | solution.py:22
  236.7 12.2 %all_to_all.77 = f32[8,32,256]{2,1,0:T(8,128)} all-to-all(f32[8,32,256]{2,1,0:T(8,128)S(1)} %broadcast_in_dim.165), channel_id=1, replica_groups=mesh['grp'=8,'z'=8,'x'=4,'core'=2] {'x','core'}, dimensions={0} | all-to-all | bytes 524288 | tf_op jit(solution)/shard_map/all_to_all | solution.py:22
  250.1 13.4 %all_to_all.78 = f32[8,32,256]{2,1,0:T(8,128)} all-to-all(f32[8,32,256]{2,1,0:T(8,128)S(1)} %broadcast_in_dim.166), channel_id=1, replica_groups=mesh['grp'=8,'z'=8,'x'=4,'core'=2] {'grp'}, dimensions={0} | all-to-all | bytes 524288 | tf_op jit(solution)/shard_map/all_to_all | solution.py:22
  264.7 11.4 %all_to_all.79 = f32[8,32,256]{2,1,0:T(8,128)S(1)} all-to-all(f32[8,32,256]{2,1,0:T(8,128)S(1)} %broadcast_in_dim.167), channel_id=1, replica_groups=mesh['grp'=8,'z'=8,'x'=4,'core'=2] {'x','core'}, dimensions={0} | all-to-all | bytes 524288 | tf_op jit(solution)/shard_map/all_to_all | solution.py:22
  276.4 12.7 %all_to_all.80 = f32[8,32,256]{2,1,0:T(8,128)S(1)} all-to-all(f32[8,32,256]{2,1,0:T(8,128)S(1)} %broadcast_in_dim.168), channel_id=1, replica_groups=mesh['grp'=8,'z'=8,'x'=4,'core'=2] {'grp'}, dimensions={0} | all-to-all | bytes 524288 | tf_op jit(solution)/shard_map/all_to_all | solution.py:22
  289.3 14.2 %all_to_all.81 = f32[8,32,512]{2,1,0:T(8,128)S(1)} all-to-all(f32[8,32,512]{2,1,0:T(8,128)S(1)} %broadcast_in_dim.169), channel_id=1, replica_groups=mesh['grp'=8,'z'=8,'x'=4,'core'=2] {'x','core'}, dimensions={0} | all-to-all | bytes 1048576 | tf_op jit(solution)/shard_map/all_to_all | solution.py:22
  305.4 4.1 %copy.87 = f32[32,2,8,8,32]{4,3,2,1,0:T(8,128)} copy(f32[32,2,8,8,32]{4,2,1,0,3:T(8,128)} %bitcast.113) | data formatting | bytes 1048576 | tf_op jit(solution)/shard_map/transpose | solution.py:117
  313.2 5.7 %all-to-all-start.13 = ((f32[64,8,128]{2,1,0:T(8,128)}), f32[64,8,128]{2,1,0:T(8,128)S(1)}, u32[]{:S(2)}, u32[]{:S(2)}) async-start(f32[64,8,128]{2,1,0:T(8,128)} %broadcast_in_dim.171), calls=%async_computation.13 | async-start | bytes 524288 | tf_op jit(solution)/shard_map/all_to_all | solution.py:22
  320.2 11.9 %all-to-all-done.13 = f32[64,8,128]{2,1,0:T(8,128)S(1)} async-done(((f32[64,8,128]{2,1,0:T(8,128)}), f32[64,8,128]{2,1,0:T(8,128)S(1)}, u32[]{:S(2)}, u32[]{:S(2)}) %all-to-all-start.13) | async-done | bytes 262176 | tf_op jit(solution)/shard_map/all_to_all | solution.py:22
  339.6 3.6 %all-to-all-start.14 = ((f32[8,32,256]{2,1,0:T(8,128)}), f32[8,32,256]{2,1,0:T(8,128)S(1)}, u32[]{:S(2)}, u32[]{:S(2)}) async-start(f32[8,32,256]{2,1,0:T(8,128)} %broadcast_in_dim.172), calls=%async_computation.14 | async-start | bytes 524288 | tf_op jit(solution)/shard_map/all_to_all | solution.py:22
  344.1 5.7 %all-to-all-done.14 = f32[8,32,256]{2,1,0:T(8,128)S(1)} async-done(((f32[8,32,256]{2,1,0:T(8,128)}), f32[8,32,256]{2,1,0:T(8,128)S(1)}, u32[]{:S(2)}, u32[]{:S(2)}) %all-to-all-start.14) | async-done | bytes 262176 | tf_op jit(solution)/shard_map/all_to_all | solution.py:22
  (132 shorter events, 63.3 us)
Async XLA Ops:
  0.6 138.6 %copy-start = (f32[32,4096]{1,0:T(8,128)S(1)}, f32[32,4096]{1,0:T(8,128)}, u32[]{:S(2)}) copy-start(f32[32,4096]{1,0:T(8,128)} %param.22) | copy-start | bytes 1572868
  8.6 1.0 copy-start.8
  10.5 11.4 %copy-start.16 = (f32[32,32]{1,0:T(8,128)S(1)}, f32[32,32]{1,0:T(8,128)}, u32[]{:S(2)}) copy-start(f32[32,32]{1,0:T(8,128)} %param.20) | copy-start | bytes 12292
  10.7 24.1 %copy-start.7 = (f32[32,2048]{1,0:T(8,128)S(1)}, f32[32,2048]{1,0:T(8,128)}, u32[]{:S(2)}) copy-start(f32[32,2048]{1,0:T(8,128)} %param.21) | copy-start | bytes 786436
  10.7 24.1 %copy-start.13 = (f32[2,32,256]{2,1,0:T(8,128)S(1)}, f32[2,32,256]{2,1,0:T(8,128)}, u32[]{:S(2)}) copy-start(f32[2,32,256]{2,1,0:T(8,128)} %param.24) | copy-start | bytes 196612
  10.8 24.1 %copy-start.14 = (f32[1,32,256]{2,1,0:T(8,128)S(1)}, f32[1,32,256]{2,1,0:T(8,128)}, u32[]{:S(2)}) copy-start(f32[1,32,256]{2,1,0:T(8,128)} %param.25) | copy-start | bytes 98308
  11.8 16.6 %all-to-all-start = ((f32[8,32,256]{2,1,0:T(8,128)}), f32[8,32,256]{2,1,0:T(8,128)S(1)}, u32[]{:S(2)}, u32[]{:S(2)}) async-start(f32[8,32,256]{2,1,0:T(8,128)} %reshape.163), calls=%async_computation | async-start | bytes 524288 | tf_op jit(solution)/shard_map/all_to_all | solution.py:22
  29.2 15.8 %all-to-all-start.1 = ((f32[8,32,256]{2,1,0:T(8,128)}), f32[8,32,256]{2,1,0:T(8,128)S(1)}, u32[]{:S(2)}, u32[]{:S(2)}) async-start(f32[8,32,256]{2,1,0:T(8,128)} %broadcast_in_dim.159), calls=%async_computation.1 | async-start | bytes 524288 | tf_op jit(solution)/shard_map/all_to_all | solution.py:22
  47.0 69.2 %all-to-all-start.2 = ((f32[8,11,32,256]{3,2,1,0:T(8,128)}), f32[8,11,32,256]{3,2,1,0:T(8,128)}, u32[]{:S(2)}, u32[]{:S(2)}) async-start(f32[8,11,32,256]{3,2,1,0:T(8,128)} %stack.8), calls=%async_computation.2 | async-start | bytes 5767168 | tf_op jit(solution)/shard_map/all_to_all | solution.py:74
  125.1 14.0 %all-to-all-start.3 = ((f32[8,32,256]{2,1,0:T(8,128)}), f32[8,32,256]{2,1,0:T(8,128)S(1)}, u32[]{:S(2)}, u32[]{:S(2)}) async-start(f32[8,32,256]{2,1,0:T(8,128)} %reshape.167), calls=%async_computation.3 | async-start | bytes 524288 | tf_op jit(solution)/shard_map/all_to_all | solution.py:22
  139.2 5.6 %copy-start.10 = (f32[32,256]{1,0:T(8,128)}, f32[32,256]{1,0:T(8,128)S(1)}, u32[]{:S(2)}) copy-start(f32[32,256]{1,0:T(8,128)S(1)} %reduce_sum.107) | copy-start | bytes 98308
  144.8 7.5 %copy-start.15 = (f32[32,2,32]{2,1,0:T(2,128)S(1)}, f32[32,2,32]{2,1,0:T(2,128)}, u32[]{:S(2)}) copy-start(f32[32,2,32]{2,1,0:T(2,128)} %param.23) | copy-start | bytes 24580
  147.2 22.9 %all-to-all-start.4 = ((f32[64,16,128]{2,1,0:T(8,128)}), f32[64,16,128]{2,1,0:T(8,128)S(1)}, u32[]{:S(2)}, u32[]{:S(2)}) async-start(f32[64,16,128]{2,1,0:T(8,128)} %copy.85), calls=%async_computation.4 | async-start | bytes 1048576 | tf_op jit(solution)/shard_map/all_to_all | solution.py:22
  171.1 26.3 %all-to-all-start.5 = ((f32[64,16,128]{2,1,0:T(8,128)}), f32[64,16,128]{2,1,0:T(8,128)}, u32[]{:S(2)}, u32[]{:S(2)}) async-start(f32[64,16,128]{2,1,0:T(8,128)} %broadcast_in_dim.162), calls=%async_computation.5 | async-start | bytes 1048576 | tf_op jit(solution)/shard_map/all_to_all | solution.py:22
  217.2 14.2 %copy-start.5 = (f32[32,256]{1,0:T(8,128)}, f32[32,256]{1,0:T(8,128)S(1)}, u32[]{:S(2)}) copy-start(f32[32,256]{1,0:T(8,128)S(1)} %reduce_sum.110) | copy-start | bytes 98308
  236.4 39.7 %copy-start.6 = (f32[32,256]{1,0:T(8,128)S(1)}, f32[32,256]{1,0:T(8,128)}, u32[]{:S(2)}) copy-start(f32[32,256]{1,0:T(8,128)} %copy-done.5) | copy-start | bytes 98308
  309.5 2.6 copy-start.11
  313.2 18.8 %all-to-all-start.13 = ((f32[64,8,128]{2,1,0:T(8,128)}), f32[64,8,128]{2,1,0:T(8,128)S(1)}, u32[]{:S(2)}, u32[]{:S(2)}) async-start(f32[64,8,128]{2,1,0:T(8,128)} %broadcast_in_dim.171), calls=%async_computation.13 | async-start | bytes 524288 | tf_op jit(solution)/shard_map/all_to_all | solution.py:22
  339.6 10.1 %all-to-all-start.14 = ((f32[8,32,256]{2,1,0:T(8,128)}), f32[8,32,256]{2,1,0:T(8,128)S(1)}, u32[]{:S(2)}, u32[]{:S(2)}) async-start(f32[8,32,256]{2,1,0:T(8,128)} %broadcast_in_dim.172), calls=%async_computation.14 | async-start | bytes 524288 | tf_op jit(solution)/shard_map/all_to_all | solution.py:22
  344.1 7.1 %copy-start.2 = (f32[2,128,128]{2,1,0:T(8,128)S(1)}, f32[2,128,128]{2,1,0:T(8,128)}, u32[]{:S(2)}) copy-start(f32[2,128,128]{2,1,0:T(8,128)} %param.16) | copy-start | bytes 393220
  344.1 7.1 %copy-start.9 = (f32[32,128]{1,0:T(8,128)S(1)}, f32[32,128]{1,0:T(8,128)}, u32[]{:S(2)}) copy-start(f32[32,128]{1,0:T(8,128)} %copy-done.8) | copy-start | bytes 49156
  344.1 7.2 %copy-start.3 = (f32[2,128,128]{2,1,0:T(8,128)S(1)}, f32[2,128,128]{2,1,0:T(8,128)}, u32[]{:S(2)}) copy-start(f32[2,128,128]{2,1,0:T(8,128)} %param.14) | copy-start | bytes 393220
  350.0 1.7 copy-start.12
  351.2 1.6 copy-start.4
  (1 other events, 0.7 us)
